TPU v7x, 32 devices: a whole 2x2x4 slice. The times are simulated.
32 devices in a mesh: ctx: 4 (over z), ep: 8 (over y, x, core).
Axes of the slice: x: 2, y: 2, z: 4, core: 2. Of those that a mesh axis runs over, the one named last changes fastest.
Arguments:
- out_grad: bfloat16 [64, 3584], P(('ctx', 'ep')), may hold values from -6 to 6
- expert_ids: int32 [64, 8], P(('ctx', 'ep')), may hold values from 0 to 31, all different within a row; in each aligned block of 16 rows (0 to 15, 16 to 31, ...) at most 7 rows name the same one
- gate_values: float32 [64, 8], P(('ctx', 'ep')), may hold values from 0.1 to 2.5
- hidden: bfloat16 [4, 32, 7, 1536], P(None, 'ep', None, 'ctx'), may hold values from -0.29882812 to 0.29882812
- w_down: bfloat16 [32, 1536, 3584], P('ep', 'ctx'), may hold values from -0.15625 to 0.15625
Outputs:
- hidden_grad: bfloat16 [4, 32, 7, 1536], P(None, 'ep', None, 'ctx')
- weight_grad: bfloat16 [32, 1536, 3584], P('ep', 'ctx')
- gate_grad: float32 [64, 8], P(('ctx', 'ep'))
Inputs may be any that keep to these rules, and one draw needn't show every extreme that they name: `expert_ids`: each token names 8 different experts. In each aligned block of 16 tokens no expert is named by more than 7 tokens.
All inputs are finite; a program needn't handle non-finite values.
Results may differ from a plain program's by a relative error of at most 0.012.
Values may be sent and summed in bfloat16 or wider, within the bound.
A program may use at most 64 MiB of HBM per device.

v0:
```python
import jax
import jax.numpy as jnp
from jax import lax
from jax.sharding import PartitionSpec as P


def route_places(group_ids, experts_all, capacity):
    flat_ids = group_ids.reshape(-1)
    onehot = (flat_ids[:, None] == jnp.arange(experts_all, dtype=jnp.int32)[None, :]).astype(
        jnp.int32
    )
    before = jnp.cumsum(onehot, axis=0) - onehot
    slot_index = jnp.sum(before * onehot, axis=1)
    return (flat_ids * capacity + slot_index).astype(jnp.int32)


def per_device(out_grad, expert_ids, gate_values, hidden, w_down):
    tok_dev, top_count = expert_ids.shape
    groups, exp_dev, capacity, width_part = hidden.shape
    model_width = out_grad.shape[1]
    ep_count = lax.axis_size("ep")
    ep_rank = lax.axis_index("ep")
    slots_dev = exp_dev * capacity
    experts_all = exp_dev * ep_count
    own_first = ep_rank * slots_dev
    slot_range = jnp.arange(slots_dev, dtype=jnp.int32)
    group_rows, group_ids, group_gates = (
        lax.all_gather(out_grad, "ep", axis=0, tiled=True),
        lax.all_gather(expert_ids, "ep", axis=0, tiled=True),
        lax.all_gather(gate_values.astype(jnp.bfloat16), "ep", axis=0, tiled=True).astype(
            gate_values.dtype
        ),
    )
    places = route_places(group_ids, experts_all, capacity)
    own_places = lax.dynamic_slice_in_dim(
        places, ep_rank * tok_dev * top_count, tok_dev * top_count
    )
    local_slot = places - own_first
    pick_mask = (local_slot[None, :] == slot_range[:, None]).astype(jnp.float32)
    slot_gates = jnp.sum(pick_mask * group_gates.reshape(1, -1), axis=1)
    by_token = pick_mask.reshape(slots_dev, -1, top_count).sum(axis=2).astype(jnp.bfloat16)
    slot_rows = jnp.dot(by_token, group_rows, preferred_element_type=jnp.float32).astype(
        jnp.bfloat16
    )
    stacked_rows = slot_rows.reshape(1, slots_dev, model_width)
    stacked_gates = slot_gates.reshape(1, slots_dev)
    whole_rows, whole_gates = (
        lax.all_gather(stacked_rows, "ctx", axis=0, tiled=True),
        lax.all_gather(stacked_gates.astype(jnp.bfloat16), "ctx", axis=0, tiled=True).astype(
            stacked_gates.dtype
        ),
    )
    row_count = whole_rows.shape[0]
    piece_view = whole_rows.reshape(row_count, exp_dev, capacity, model_width)
    gate_view = whole_gates.reshape(row_count, exp_dev, capacity)
    grad_in = jnp.einsum("necd,efd->necf", piece_view, w_down, preferred_element_type=jnp.float32)
    hid_piece = (gate_view[..., None] * grad_in).astype(jnp.bfloat16)
    gate_piece = jnp.sum(hidden.astype(jnp.float32) * grad_in, axis=3)
    scaled = (gate_view[..., None] * piece_view.astype(jnp.float32)).astype(jnp.bfloat16)
    grad_acc = jnp.einsum("necf,necd->efd", hidden, scaled, preferred_element_type=jnp.float32)
    hid_grad = hid_piece
    partial_value = gate_piece
    grad_acc, hid_grad, partial_value = (grad_acc, hid_grad, partial_value)
    whole_terms = lax.psum(partial_value, "ctx")
    own_terms = lax.dynamic_slice_in_dim(whole_terms, lax.axis_index("ctx"), 1, 0)
    score_table = lax.all_gather(own_terms.reshape(slots_dev), "ep", axis=0, tiled=True)
    lookup = (
        own_places[:, None] == jnp.arange(score_table.shape[0], dtype=jnp.int32)[None, :]
    ).astype(jnp.float32)
    gate_grad = jnp.sum(lookup * score_table[None, :], axis=1).reshape(tok_dev, top_count)
    return (hid_grad, grad_acc.astype(jnp.bfloat16), gate_grad)


def solution(mesh):
    placed = (
        P(("ctx", "ep"), None),
        P(("ctx", "ep"), None),
        P(("ctx", "ep"), None),
        P(None, "ep", None, "ctx"),
        P("ep", "ctx", None),
    )
    return jax.shard_map(
        per_device,
        mesh=mesh,
        in_specs=placed,
        out_specs=(P(None, "ep", None, "ctx"), P("ep", "ctx", None), P(("ctx", "ep"), None)),
        check_vma=False,
    )
```

profile of v0, /device:TPU:0, one launch (start us, length us, event | category | flops | bytes accessed | tf_op | source)
XLA Modules:
  0.0 119.2 jit_solution(10232744558941915128)
XLA Ops:
  0.7 1.3 %dynamic-slice.1 = u32[1]{0:T(128)} dynamic-slice(u32[32]{0:T(128)} %constant.42, u32[]{:T(128)S(6)} %add.22), dynamic_slice_sizes={1} | dynamic-slice | bytes 12
  2.6 1.2 %dynamic-slice = u32[1]{0:T(128)} dynamic-slice(u32[32]{0:T(128)} %constant.37, u32[]{:T(128)S(6)} %add.22), dynamic_slice_sizes={1} | dynamic-slice | bytes 12
  4.5 0.7 convert_bitcast_fusion
  5.2 10.3 %all-gather.3 = bf16[8,2,8]{2,1,0:T(2,128)(2,1)S(1)} all-gather(bf16[1,2,8]{2,1,0:T(2,128)(2,1)S(1)} %convert_bitcast_fusion), channel_id=1, replica_groups=mesh['ctx'=4,'ep'=8] {'ep'}, dimensions={0}, use_global_device_ids=true | all-gather | bytes 288 | tf_op jit(solution)/shard_map/all_gather | solution.py:30
  15.4 0.1 reshape.61
  15.5 8.9 %all-gather.2 = s32[8,2,8]{2,1,0:T(2,128)S(1)} all-gather(s32[1,2,8]{2,1,0:T(2,128)} %bitcast.35), channel_id=1, replica_groups=mesh['ctx'=4,'ep'=8] {'ep'}, dimensions={0}, use_global_device_ids=true | all-gather | bytes 576 | tf_op jit(solution)/shard_map/all_gather | solution.py:29
  24.4 0.1 reshape.56
  24.5 0.1 fusion.9
  24.6 0.2 reduce_window_sum.11
  24.8 0.2 select_reduce_fusion
  25.0 0.1 select_reduce_fusion.2
  25.1 0.2 dynamic-update-slice
  25.4 11.9 %all-reduce = bf16[112]{0:T(256)(128)(2,1)S(1)} all-reduce(bf16[112]{0:T(256)(128)(2,1)S(1)} %dynamic-update-slice), channel_id=2, replica_groups=mesh['ctx'=4,'ep'=8] {'ctx'}, use_global_device_ids=true, to_apply=%add | all-reduce | flops 112 | bytes 448
  37.4 0.1 reshape.62
  37.5 0.1 reduce_sum.49
  37.6 0.1 convert_reduce_fusion
  37.7 0.1 copy.33
  37.8 8.4 %all-gather.4 = bf16[8,2,3584]{2,1,0:T(2,128)(2,1)S(1)} all-gather(bf16[1,2,3584]{2,1,0:T(2,128)(2,1)} %bitcast.34), channel_id=1, replica_groups=mesh['ctx'=4,'ep'=8] {'ep'}, dimensions={0}, use_global_device_ids=true | all-gather | bytes 129024 | tf_op jit(solution)/shard_map/all_gather | solution.py:28
  46.3 0.2 fusion.3
  46.5 19.8 %all-gather.5 = bf16[4,28,3584]{2,1,0:T(8,128)(2,1)S(1)} all-gather(bf16[1,28,3584]{2,1,0:T(8,128)(2,1)S(1)} %fusion.3), channel_id=3, replica_groups=mesh['ctx'=4,'ep'=8] {'ctx'}, dimensions={0}, use_global_device_ids=true | all-gather | bytes 1003520 | tf_op jit(solution)/shard_map/all_gather | solution.py:48
  66.3 0.6 copy.34
  67.0 7.6 %multiply_reduce_fusion = (f32[4,4,7]{0,2,1:T(8,128)S(1)}, bf16[4,4,7,384]{3,0,2,1:T(4,128)(2,1)S(1)}) fusion(bf16[4,4,7,384]{3,1,2,0:T(4,128)(2,1)} %param.8, f32[4,4,7]{0,2,1:T(8,128)S(1)} %copy.33, bf16[4,4,7,3584]{3,0,2,1:T(4,128)(2,1)S(1)} %bitcast.31, bf16[4,384,3584]{2,1,0:T(8,128)(2,1)} %param.9), kind=kOutput, calls=%fused_computation.9 | convolution fusion | flops 308496256 | bytes 11985792 | tf_op jit(solution)/shard_map/necd,efd->necf/dot_general | solution.py:56
  74.6 0.1 copy.43
  74.7 10.0 %psum.7 = f32[4,4,7]{2,0,1:T(4,128)S(1)} all-reduce(f32[4,4,7]{2,0,1:T(4,128)S(1)} %copy.43), channel_id=1, replica_groups=mesh['ctx'=4,'ep'=8] {'ctx'}, use_global_device_ids=true, to_apply=%region_5.6 | all-reduce | flops 112 | bytes 896 | tf_op jit(solution)/shard_map/psum | solution.py:64
  84.7 0.1 reshape.71
  84.7 0.2 dynamic-update-slice.1
  84.9 11.8 %all-reduce.1 = f32[224]{0:T(256)S(1)} all-reduce(f32[224]{0:T(256)S(1)} %dynamic-update-slice.1), channel_id=1, replica_groups=mesh['ctx'=4,'ep'=8] {'ep'}, use_global_device_ids=true, to_apply=%add.1 | all-reduce | flops 224 | bytes 1792
  96.7 0.2 select_reduce_fusion.1
  96.9 0.6 reshape.60
  97.5 0.7 copy.39
  98.2 6.3 %fusion = bf16[4,384,3584]{1,2,0:T(8,128)(2,1)} fusion(bf16[4,4,7,3584]{3,0,2,1:T(4,128)(2,1)S(1)} %bitcast.32, f32[4,4,7]{0,2,1:T(8,128)S(1)} %copy.33, bf16[4,4,7,384]{3,1,2,0:T(4,128)(2,1)S(1)} %copy-done), kind=kOutput, calls=%fused_computation.1 | convolution fusion | flops 314990592 | bytes 11899328 | tf_op jit(solution)/shard_map/necf,necd->efd/dot_general | solution.py:60
  104.6 14.6 %copy.40 = bf16[4,384,3584]{2,1,0:T(8,128)(2,1)} copy(bf16[4,384,3584]{1,2,0:T(8,128)(2,1)} %fusion) | data formatting | bytes 22020096
  (10 shorter events, 0.2 us)
Async XLA Ops:
  0.6 97.6 %copy-start = (bf16[4,4,7,384]{3,1,2,0:T(4,128)(2,1)S(1)}, bf16[4,4,7,384]{3,1,2,0:T(4,128)(2,1)}, u32[]{:S(2)}) copy-start(bf16[4,4,7,384]{3,1,2,0:T(4,128)(2,1)} %param.8) | copy-start | bytes 258052
where the time goes:
time: 120 us; the launch traced here: 119 us
  blocking collectives  81.1 us (68%)
  local copies, waits for them, and re-layouts  20.3 us (17%)
  matrix products  14.2 us (12%)
  between operations  2.04 us (2%)
  other arithmetic  1.55 us (1%)
    unnamed x2, blocking collectives  23.7 us
    all_gather x1, blocking collectives, per_device(): lax.all_gather(stacked_rows, 'ctx', axis=0, tiled=True)  19.8 us
    unnamed x12, local copies, waits for them, and re-layouts  18.4 us
    all_gather x1, blocking collectives, per_device(): lax.all_gather(gate_values.astype(jnp.bfloat16), 'ep', axis=0, tiled=True)  10.3 us
    psum x1, blocking collectives, per_device(): whole_terms = lax.psum(partial_value, 'ctx')  9.95 us
    all_gather x1, blocking collectives, per_device(): lax.all_gather(expert_ids, 'ep', axis=0, tiled=True)  8.91 us
    all_gather x1, blocking collectives, per_device(): lax.all_gather(out_grad, 'ep', axis=0, tiled=True)  8.44 us
    dot_general x1, matrix products, per_device(): jnp.einsum('necd,efd->necf', piece_view, w_down, preferred_element_type=j...  7.58 us

commit v1 on v0

--- a/solution.py
+++ b/solution.py
@@ -61,7 +61,11 @@
     hid_grad = hid_piece
     partial_value = gate_piece
     grad_acc, hid_grad, partial_value = (grad_acc, hid_grad, partial_value)
-    whole_terms = lax.psum(partial_value, "ctx")
+    whole_terms = partial_value
+    for hop in (1, 2):
+        whole_terms = whole_terms + lax.ppermute(
+            whole_terms, "ctx", [(dev, dev ^ hop) for dev in range(4)]
+        )
     own_terms = lax.dynamic_slice_in_dim(whole_terms, lax.axis_index("ctx"), 1, 0)
     score_table = lax.all_gather(own_terms.reshape(slots_dev), "ep", axis=0, tiled=True)
     lookup = (

time: 120 us -> 111 us (0.925)
  blocking collectives: 81.1 us -> 71.3 us
  starting transfers between devices: 0 us -> 2.11 us
    psum x1 -> x0, blocking collectives: 9.95 us -> none  [per_device(): whole_terms = lax.psum(partial_value, 'ctx')]
    ppermute x0 -> x2, starting transfers between devices: none -> 2.11 us  [per_device(): lax.ppermute(whole_terms, 'ctx', [(dev, dev ^ hop) for dev in range(4)])]
    all_gather x1, blocking collectives: 8.91 us -> 10.7 us  [per_device(): lax.all_gather(expert_ids, 'ep', axis=0, tiled=True)]
    all_gather x1, blocking collectives: 10.3 us -> 8.61 us  [per_device(): lax.all_gather(gate_values.astype(jnp.bfloat16), 'ep', axis=0, tiled=True)]
    unnamed x12 -> x14, local copies, waits for them, and re-layouts: 18.4 us -> 17.7 us
  transfers between devices with their start and end apart: 0 -> 2, of which waited for: 0 -> 0; matrix products, arithmetic and copies ran while one was open for 0% -> 20% of each run, Pallas kernels for 0% -> 0%
where the time goes in v1:
time: 111 us
  blocking collectives  71.3 us (64%)
  local copies, waits for them, and re-layouts  19.6 us (18%)
  matrix products  14.1 us (13%)
  starting transfers between devices  2.11 us (2%)
  between operations  2.06 us (2%)
  other arithmetic  1.58 us (1%)
    unnamed x2, blocking collectives  23.7 us
    all_gather x1, blocking collectives, per_device(): lax.all_gather(stacked_rows, 'ctx', axis=0, tiled=True)  19.8 us
    unnamed x14, local copies, waits for them, and re-layouts  17.7 us
    all_gather x1, blocking collectives, per_device(): lax.all_gather(expert_ids, 'ep', axis=0, tiled=True)  10.7 us
    all_gather x1, blocking collectives, per_device(): lax.all_gather(gate_values.astype(jnp.bfloat16), 'ep', axis=0, tiled=True)  8.61 us
    all_gather x1, blocking collectives, per_device(): lax.all_gather(out_grad, 'ep', axis=0, tiled=True)  8.44 us
    dot_general x1, matrix products, per_device(): jnp.einsum('necd,efd->necf', piece_view, w_down, preferred_element_type=j...  7.55 us
    dot_general x1, matrix products, per_device(): jnp.einsum('necf,necd->efd', hidden, scaled, preferred_element_type=jnp.f...  6.35 us
  transfers between devices with their start and end apart: 2, of which 0 were waited for; matrix products, arithmetic and copies ran while one was open for 20% of the time, Pallas kernels for 0%

profile of v1, /device:TPU:0, one launch (start us, length us, event | category | flops | bytes accessed | tf_op | source)
XLA Modules:
  0.0 110.8 jit_solution(6288515360543474448)
XLA Ops:
  0.6 10.7 %all-gather.2 = s32[8,2,8]{2,1,0:T(2,128)S(1)} all-gather(s32[1,2,8]{2,1,0:T(2,128)} %bitcast.35), channel_id=1, replica_groups=mesh['ctx'=4,'ep'=8] {'ep'}, dimensions={0}, use_global_device_ids=true | all-gather | bytes 576 | tf_op jit(solution)/shard_map/all_gather | solution.py:29
  11.3 0.1 reshape.56
  11.5 0.7 convert_bitcast_fusion
  12.1 8.6 %all-gather.3 = bf16[8,2,8]{2,1,0:T(2,128)(2,1)S(1)} all-gather(bf16[1,2,8]{2,1,0:T(2,128)(2,1)S(1)} %convert_bitcast_fusion), channel_id=1, replica_groups=mesh['ctx'=4,'ep'=8] {'ep'}, dimensions={0}, use_global_device_ids=true | all-gather | bytes 288 | tf_op jit(solution)/shard_map/all_gather | solution.py:30
  20.8 0.1 reshape.61
  20.8 0.1 fusion.9
  20.9 0.2 reduce_window_sum.11
  21.1 0.2 select_reduce_fusion
  21.3 0.1 reduce_sum.49
  21.4 1.2 %dynamic-slice = u32[1]{0:T(128)} dynamic-slice(u32[32]{0:T(128)} %constant.37, u32[]{:T(128)S(6)} %add.28), dynamic_slice_sizes={1} | dynamic-slice | bytes 12
  23.3 0.1 select_reduce_fusion.2
  23.4 0.2 dynamic-update-slice
  23.6 11.9 %all-reduce = bf16[112]{0:T(256)(128)(2,1)S(1)} all-reduce(bf16[112]{0:T(256)(128)(2,1)S(1)} %dynamic-update-slice), channel_id=2, replica_groups=mesh['ctx'=4,'ep'=8] {'ctx'}, use_global_device_ids=true, to_apply=%add | all-reduce | flops 112 | bytes 448
  35.6 0.1 reshape.62
  35.7 0.1 convert_reduce_fusion
  35.8 0.1 copy.33
  35.9 8.4 %all-gather.4 = bf16[8,2,3584]{2,1,0:T(2,128)(2,1)S(1)} all-gather(bf16[1,2,3584]{2,1,0:T(2,128)(2,1)} %bitcast.34), channel_id=1, replica_groups=mesh['ctx'=4,'ep'=8] {'ep'}, dimensions={0}, use_global_device_ids=true | all-gather | bytes 129024 | tf_op jit(solution)/shard_map/all_gather | solution.py:28
  44.4 0.2 fusion.3
  44.7 19.8 %all-gather.5 = bf16[4,28,3584]{2,1,0:T(8,128)(2,1)S(1)} all-gather(bf16[1,28,3584]{2,1,0:T(8,128)(2,1)S(1)} %fusion.3), channel_id=3, replica_groups=mesh['ctx'=4,'ep'=8] {'ctx'}, dimensions={0}, use_global_device_ids=true | all-gather | bytes 1003520 | tf_op jit(solution)/shard_map/all_gather | solution.py:48
  64.5 0.6 copy.34
  65.1 7.6 %multiply_reduce_fusion = (f32[4,4,7]{0,2,1:T(8,128)S(1)}, bf16[4,4,7,384]{3,0,2,1:T(4,128)(2,1)S(1)}) fusion(bf16[4,4,7,384]{3,1,2,0:T(4,128)(2,1)} %param.8, f32[4,4,7]{0,2,1:T(8,128)S(1)} %copy.33, bf16[4,4,7,3584]{3,0,2,1:T(4,128)(2,1)S(1)} %bitcast.31, bf16[4,384,3584]{2,1,0:T(8,128)(2,1)} %param.9), kind=kOutput, calls=%fused_computation.9 | convolution fusion | flops 308496256 | bytes 11985792 | tf_op jit(solution)/shard_map/necd,efd->necf/dot_general | solution.py:56
  72.7 0.1 copy.43
  72.8 6.4 %fusion = bf16[4,384,3584]{1,2,0:T(8,128)(2,1)} fusion(bf16[4,4,7,3584]{3,0,2,1:T(4,128)(2,1)S(1)} %bitcast.32, f32[4,4,7]{0,2,1:T(8,128)S(1)} %copy.33, bf16[4,4,7,384]{3,1,2,0:T(4,128)(2,1)S(1)} %copy-done), kind=kOutput, calls=%fused_computation.1 | convolution fusion | flops 314990592 | bytes 11899328 | tf_op jit(solution)/shard_map/necf,necd->efd/dot_general | solution.py:60
  79.2 2.1 %collective-permute-start.1 = (f32[4,4,7]{2,0,1:T(4,128)S(1)}, f32[4,4,7]{2,0,1:T(4,128)S(1)}, u32[]{:S(2)}, u32[]{:S(2)}) collective-permute-start(f32[4,4,7]{2,0,1:T(4,128)S(1)} %add.25), channel_id=1, source_target_pairs={{0,16},{8,24},{16,0},{24,8},{1,17},{9,25},{17,1},{25,9},{2,18},{10... | collective-permute-start | bytes 1352 | tf_op jit(solution)/shard_map/ppermute | solution.py:66
  81.3 0.6 dynamic-slice.1
  82.5 0.7 copy.39
  83.2 14.6 %copy.40 = bf16[4,384,3584]{2,1,0:T(8,128)(2,1)} copy(bf16[4,384,3584]{1,2,0:T(8,128)(2,1)} %fusion) | data formatting | bytes 22020096
  97.9 0.1 reshape.71
  98.0 0.2 dynamic-update-slice.1
  98.2 11.8 %all-reduce.1 = f32[224]{0:T(256)S(1)} all-reduce(f32[224]{0:T(256)S(1)} %dynamic-update-slice.1), channel_id=1, replica_groups=mesh['ctx'=4,'ep'=8] {'ep'}, use_global_device_ids=true, to_apply=%add.1 | all-reduce | flops 224 | bytes 1792
  110.0 0.2 select_reduce_fusion.1
  110.2 0.6 reshape.60
  (16 shorter events, 0.2 us)
Async XLA Ops:
  0.6 72.2 %copy-start = (bf16[4,4,7,384]{3,1,2,0:T(4,128)(2,1)S(1)}, bf16[4,4,7,384]{3,1,2,0:T(4,128)(2,1)}, u32[]{:S(2)}) copy-start(bf16[4,4,7,384]{3,1,2,0:T(4,128)(2,1)} %param.8) | copy-start | bytes 258052
  72.8 8.5 %copy-start.1 = (u32[32]{0:T(128)S(1)}, u32[32]{0:T(128)}, u32[]{:S(2)}) copy-start(u32[32]{0:T(128)} %constant.42) | copy-start | bytes 388
  72.8 6.4 %collective-permute-start = (f32[4,4,7]{2,0,1:T(4,128)S(1)}, f32[4,4,7]{2,0,1:T(4,128)S(1)}, u32[]{:S(2)}, u32[]{:S(2)}) collective-permute-start(f32[4,4,7]{2,0,1:T(4,128)S(1)} %copy.43), channel_id=1, source_target_pairs={{0,8},{8,0},{16,24},{24,16},{1,9},{9,1},{17,25},{25,17},{2,10},{10... | collective-permute-start | bytes 1352 | tf_op jit(solution)/shard_map/ppermute | solution.py:66
  79.2 18.7 %collective-permute-start.1 = (f32[4,4,7]{2,0,1:T(4,128)S(1)}, f32[4,4,7]{2,0,1:T(4,128)S(1)}, u32[]{:S(2)}, u32[]{:S(2)}) collective-permute-start(f32[4,4,7]{2,0,1:T(4,128)S(1)} %add.25), channel_id=1, source_target_pairs={{0,16},{8,24},{16,0},{24,8},{1,17},{9,25},{17,1},{25,9},{2,18},{10... | collective-permute-start | bytes 1352 | tf_op jit(solution)/shard_map/ppermute | solution.py:66
